TPU v7x, 256 devices: a whole 4x4x8 slice. The times are simulated.
256 devices in a mesh: rec: 32 (over z, x), ani: 4 (over y_lo, core), chain: 2 (over y_hi).
Axes of the slice: x: 4, y: 4 (y_hi: 2, y_lo: 2; y = y_hi * 2 + y_lo), z: 8, core: 2. Of those that a mesh axis runs over, the one named last changes fastest.
Arguments:
- genotypes: bfloat16 [131072, 4096], P('ani', 'rec'), may hold values from -0.09375 to 0.09375
- effects: float32 [8192], P(('chain', 'rec')), parts along dimension 0, may hold values from -6 to 6
- gaussian_draw: float32 [8192], P(('chain', 'rec')), parts along dimension 0, may hold values from -6 to 6
- prior_prec: float32 [4096], P('rec'), may hold values from 2 to 40
- accept: int32 [64], P(('chain', 'rec')), parts along dimension 0, may hold values 0 or 1
- herd_effect: float32 [131072], P(('chain', 'rec')), parts along dimension 0, may hold values from -6 to 6
- phenotype: float32 [1048576], P(('rec', 'ani')), may hold values from -12 to 12
- record_animal: int32 [1048576], P(('rec', 'ani')), may hold values from 0 to 131071
- record_bin: int32 [1048576], P(('rec', 'ani')), may hold values from 0 to 65535, as said below
- live_records: int32 [128], P(('rec', 'ani')), may hold values from 1 to 8192, 655360 in all
Outputs:
- next_effects: float32 [8192], P(('chain', 'rec')), parts along dimension 0
- resid_sum: float32 [262144], P(('chain', 'ani')), parts along dimension 0
There are 2 independent parts, one for each index of `chain`. A program takes and returns all parts, laid end to end along the dimension named above; an argument that names none is the same for every part. Nothing has to cross between parts.
Inputs may be any that keep to these rules, and one draw needn't show every extreme that they name: `record_bin`: a record held by rec index k names a group of k * 2048 to (k + 1) * 2048 - 1.
All inputs are finite; a program needn't handle non-finite values. No bound on the sum of `accept` or of `live_records` on one device may be relied on, other than what follows from the above.
Results may differ from a plain program's by a relative error of at most 0.0033.
Values sent between devices are 32-bit elements; how exact they have to be, the bound alone decides.
A program may use at most 64 MiB of HBM per device.

v0:
```python
import math
import jax
import jax.numpy as jnp
from jax import lax
from jax.sharding import PartitionSpec as P

BLOCK = 128


def on_device(
    genotypes,
    effects,
    gaussian_draw,
    prior_prec,
    accept,
    herd_effect,
    phenotype,
    record_animal,
    record_bin,
    live_records,
):
    step_size = 0.005
    effects_half = effects.astype(jnp.bfloat16)
    partial_value = jnp.dot(genotypes, effects_half, preferred_element_type=jnp.float32)
    breeding_block = lax.psum(partial_value, "rec")
    breeding = lax.all_gather(breeding_block, "ani", axis=0, tiled=True)
    local_bin = record_bin - lax.axis_index("rec") * herd_effect.shape[0]
    position = jnp.arange(phenotype.shape[0], dtype=jnp.int32)
    live = position < live_records[0]
    herd_value = jnp.take(herd_effect, local_bin)
    residual = jnp.where(
        live, phenotype - herd_value - jnp.take(breeding, record_animal), jnp.zeros_like(phenotype)
    )
    animals = breeding.shape[0]
    partial_sums = jax.ops.segment_sum(residual, record_animal, num_segments=animals)
    share = lax.psum_scatter(partial_sums, "ani", scatter_dimension=0, tiled=True)
    resid_sum = lax.psum(share, "rec")
    resid_half = resid_sum.astype(jnp.bfloat16)
    grad_part = jnp.dot(resid_half, genotypes, preferred_element_type=jnp.float32)
    likelihood_grad = lax.psum(grad_part, "ani")
    gradient = likelihood_grad - prior_prec * effects
    proposal = effects + step_size * gradient + math.sqrt(2.0 * step_size) * gaussian_draw
    accepted = jnp.repeat(accept, BLOCK) == 1
    return (jnp.where(accepted, proposal, effects), resid_sum)


def solution(mesh):
    return jax.shard_map(
        on_device,
        mesh=mesh,
        in_specs=(
            P("ani", "rec"),
            P(("chain", "rec")),
            P(("chain", "rec")),
            P("rec"),
            P(("chain", "rec")),
            P(("chain", "rec")),
            P(("rec", "ani")),
            P(("rec", "ani")),
            P(("rec", "ani")),
            P(("rec", "ani")),
        ),
        out_specs=(P(("chain", "rec")), P(("chain", "ani"))),
        check_vma=False,
    )
```

profile of v0, /device:TPU:1, one launch (start us, length us, event | category | flops | bytes accessed | tf_op | source)
XLA Modules:
  0.0 464.9 jit_solution(7304369323534873181)
XLA Ops:
  7.2 0.0 copy-start
  7.2 0.0 copy-start.2
  7.2 0.0 all-reduce.5.cloned.1.call-start
  7.2 6.3 %fusion.4 = f32[1,32768]{1,0:T(1,128)} fusion(bf16[32768,128]{1,0:T(8,128)(2,1)} %param.10, f32[128]{0:T(128)} %param.11), kind=kOutput, calls=%fused_computation.13 | convolution fusion | flops 8388736 | bytes 8520192 | tf_op jit(solution)/shard_map/dot_general | solution.py:24
  13.5 0.0 all-reduce.5.cloned.1.call-update
  13.6 0.0 all-reduce.9.cloned.1.call-start
  14.3 0.0 copy-done.2
  14.3 0.0 copy-done
  14.3 0.0 copy-start.3
  14.3 45.5 %gather_fusion = f32[8192]{0:T(1024)S(1)} fusion(f32[2048]{0:T(1024)S(1)} %copy-done, s32[8192]{0:T(1024)S(1)} %fusion.3), kind=kCustom, calls=%fused_computation | custom fusion | bytes 98304 | tf_op jit(solution)/shard_map/jit(_take)/gather | solution.py:30
  59.9 0.0 copy-done.3
  59.9 95.9 %all-reduce.5.cloned.1.call-done = f32[32768]{0:T(1024)} async-done(((f32[32768]{0:T(1024)}), f32[32768]{0:T(1024)}) %all-reduce.5.cloned.1.call-update) | async-done | bytes 131088 | tf_op jit(solution)/shard_map/psum | solution.py:25
  155.8 12.2 %all_gather.3 = f32[131072]{0:T(1024)S(1)} all-gather(f32[32768]{0:T(1024)} %all-reduce.5.cloned.1.call-done), channel_id=1, replica_groups=mesh['rec'=32,'ani'=4,'chain'=2] {'ani'}, dimensions={0}, use_global_device_ids=true | all-gather | bytes 655360 | tf_op jit(solution)/shard_map/all_gather | solution.py:26
  167.9 0.0 copy-start.4
  167.9 0.0 copy-start.8
  167.9 45.5 %gather_fusion.1 = f32[8192]{0:T(1024)S(1)} fusion(f32[131072]{0:T(1024)S(1)} %all_gather.3, s32[8192]{0:T(1024)S(1)} %fusion.2), kind=kCustom, calls=%fused_computation.1 | custom fusion | bytes 98304 | tf_op jit(solution)/shard_map/jit(_take)/gather | solution.py:32
  213.5 0.0 copy-done.4
  213.5 44.0 %scatter_custom_fusion = f32[131072]{0:T(1024)} fusion(s32[8192]{0:T(1024)S(1)} %copy-done.3, f32[8192]{0:T(1024)S(1)} %subtract_select_fusion, f32[]{:T(128)} %constant.22.clone.1), kind=kCustom, calls=%fused_computation.4 | custom fusion | flops 8192 | bytes 524292 | tf_op jit(solution)/shard_map/scatter-add | solution.py:35
  257.5 0.0 all-reduce.9.cloned.1.call-update
  257.5 0.0 all-reduce.7.cloned.1.call-start
  257.6 0.0 copy-done.8
  257.6 0.6 dynamic-slice
  258.8 40.0 %all-reduce.9.cloned.1.call-done = f32[131072]{0:T(1024)} async-done(((f32[131072]{0:T(1024)}), f32[131072]{0:T(1024)}) %all-reduce.9.cloned.1.call-update) | async-done | bytes 524304
  298.8 1.6 dynamic-slice.1
  300.4 0.0 all-reduce.7.cloned.1.call-update
  301.0 140.5 %all-reduce.7.cloned.1.call-done = f32[32768]{0:T(1024)} async-done(((f32[32768]{0:T(1024)}), f32[32768]{0:T(1024)}) %all-reduce.7.cloned.1.call-update) | async-done | bytes 131088 | tf_op jit(solution)/shard_map/psum | solution.py:37
  441.6 0.9 convert_element_type.7
  442.5 0.1 reshape.47
  442.6 0.0 copy-start.5
  442.6 0.0 copy-start.6
  442.6 0.0 copy-start.7
  442.6 0.0 copy-start.1
  442.6 4.6 convolution_bitcast_fusion
  447.2 10.0 %psum.23 = f32[128]{0:T(128)S(1)} all-reduce(f32[128]{0:T(128)S(1)} %convolution_bitcast_fusion), channel_id=1, replica_groups=mesh['rec'=32,'ani'=4,'chain'=2] {'ani'}, use_global_device_ids=true, to_apply=%region_4.5 | all-reduce | flops 128 | bytes 1024 | tf_op jit(solution)/shard_map/psum | solution.py:40
  457.2 0.0 copy-done.5
  457.2 0.0 copy-done.6
  457.2 0.0 copy-done.7
  457.2 0.5 broadcast_select_fusion
  457.7 0.0 copy-done.1
  457.7 0.7 copy.17
  (3 shorter events, 0.1 us)
Async XLA Ops:
  7.2 7.1 %copy-start = (f32[2048]{0:T(1024)S(1)}, f32[2048]{0:T(1024)}, u32[]{:S(2)}) copy-start(f32[2048]{0:T(1024)} %param.15) | copy-start | bytes 24580
  7.2 7.1 %copy-start.2 = (s32[8192]{0:T(1024)S(1)}, s32[8192]{0:T(1024)}, u32[]{:S(2)}) copy-start(s32[8192]{0:T(1024)} %param.18) | copy-start | bytes 98308
  7.2 148.6 %all-reduce.5.cloned.1.call-start = ((), (), s32[]{:S(2)}) async-start(), calls=%async_computation | async-start | bytes 262144 | tf_op jit(solution)/shard_map/psum | solution.py:25
  13.6 285.2 %all-reduce.9.cloned.1.call-start = ((), (), s32[]{:S(2)}) async-start(), calls=%async_computation.2 | async-start | bytes 1048576
  14.3 45.6 %copy-start.3 = (s32[8192]{0:T(1024)S(1)}, s32[8192]{0:T(1024)}, u32[]{:S(2)}) copy-start(s32[8192]{0:T(1024)} %param.17) | copy-start | bytes 98308
  167.9 45.5 %copy-start.4 = (f32[8192]{0:T(1024)S(1)}, f32[8192]{0:T(1024)}, u32[]{:S(2)}) copy-start(f32[8192]{0:T(1024)} %param.16) | copy-start | bytes 98308
  167.9 89.6 %copy-start.8 = (u32[256]{0:T(256)S(1)}, u32[256]{0:T(256)}, u32[]{:S(2)}) copy-start(u32[256]{0:T(256)} %constant.51) | copy-start | bytes 3076
  257.5 184.1 %all-reduce.7.cloned.1.call-start = ((), (), s32[]{:S(2)}) async-start(), calls=%async_computation.1 | async-start | bytes 262144 | tf_op jit(solution)/shard_map/psum | solution.py:37
  442.6 14.6 %copy-start.5 = (f32[128]{0:T(128)S(1)}, f32[128]{0:T(128)}, u32[]{:S(2)}) copy-start(f32[128]{0:T(128)} %param.11) | copy-start | bytes 1540
  442.6 14.6 %copy-start.6 = (f32[128]{0:T(128)S(1)}, f32[128]{0:T(128)}, u32[]{:S(2)}) copy-start(f32[128]{0:T(128)} %param.12) | copy-start | bytes 1540
  442.6 14.6 %copy-start.7 = (f32[128]{0:T(128)S(1)}, f32[128]{0:T(128)}, u32[]{:S(2)}) copy-start(f32[128]{0:T(128)} %param.13) | copy-start | bytes 1540
  442.6 15.1 %copy-start.1 = (f32[32768]{0:T(1024)S(1)}, f32[32768]{0:T(1024)}, u32[]{:S(2)}) copy-start(f32[32768]{0:T(1024)} %all-reduce.7.cloned.1.call-done) | copy-start | bytes 393220
Sparse Core Ops, SparseCore 0:
  13.7 142.0 all-reduce.4
  257.6 41.1 all-reduce.8
  302.8 138.7 all-reduce.6
where the time goes:
time: 465 us
  waiting for transfers between devices  276 us (59%)
  local copies, waits for them, and re-layouts  94 us (20%)
  other arithmetic  45.5 us (10%)
  blocking collectives  22.1 us (5%)
  between operations  15.8 us (3%)
  matrix products  10.9 us (2%)
    psum x1, waiting for transfers between devices, on_device(): resid_sum = lax.psum(share, 'rec')  141 us
    psum x1, waiting for transfers between devices, on_device(): breeding_block = lax.psum(partial_value, 'rec')  95.9 us
    gather x1, local copies, waits for them, and re-layouts, on_device(): herd_value = jnp.take(herd_effect, local_bin)  45.5 us
    gather x1, local copies, waits for them, and re-layouts, on_device(): jnp.take(breeding, record_animal)  45.5 us
    scatter-add x1, other arithmetic, on_device(): jax.ops.segment_sum(residual, record_animal, num_segments=animals)  44 us
    unnamed x4, waiting for transfers between devices  40 us
    all_gather x1, blocking collectives, on_device(): breeding = lax.all_gather(breeding_block, 'ani', axis=0, tiled=True)  12.2 us
    psum x1, blocking collectives, on_device(): likelihood_grad = lax.psum(grad_part, 'ani')  9.98 us
  transfers between devices with their start and end apart: 3, of which 3 were waited for; matrix products, arithmetic and copies ran while one was open for 10% of the time, Pallas kernels for 0%

commit v1 on v0

--- a/solution.py
+++ b/solution.py
@@ -22,7 +22,7 @@
     step_size = 0.005
     effects_half = effects.astype(jnp.bfloat16)
     partial_value = jnp.dot(genotypes, effects_half, preferred_element_type=jnp.float32)
-    breeding_block = lax.psum(partial_value, "rec")
+    breeding_block = jnp.sum(lax.all_gather(partial_value, "rec"), axis=0)
     breeding = lax.all_gather(breeding_block, "ani", axis=0, tiled=True)
     local_bin = record_bin - lax.axis_index("rec") * herd_effect.shape[0]
     position = jnp.arange(phenotype.shape[0], dtype=jnp.int32)

time: 465 us -> 410 us (0.88)
  waiting for transfers between devices: 276 us -> 215 us
  local copies, waits for them, and re-layouts: 94 us -> 99 us
    psum x1 -> x0, waiting for transfers between devices: 95.9 us -> none  [on_device(): breeding_block = lax.psum(partial_value, 'rec')]
    all_gather x0 -> x1, waiting for transfers between devices: none -> 35.8 us  [on_device(): breeding_block = jnp.sum(lax.all_gather(partial_value, 'rec'), axis=0)]
    all_gather x0 -> x1, local copies, waits for them, and re-layouts: none -> 4.97 us  [on_device(): breeding_block = jnp.sum(lax.all_gather(partial_value, 'rec'), axis=0)]
  transfers between devices with their start and end apart: 3 -> 3, of which waited for: 3 -> 3; matrix products, arithmetic and copies ran while one was open for 10% -> 11% of each run, Pallas kernels for 0% -> 0%
where the time goes in v1:
time: 410 us
  waiting for transfers between devices  215 us (52%)
  local copies, waits for them, and re-layouts  99 us (24%)
  other arithmetic  48.1 us (12%)
  blocking collectives  21.2 us (5%)
  between operations  15.8 us (4%)
  matrix products  10.9 us (3%)
    psum x1, waiting for transfers between devices, on_device(): resid_sum = lax.psum(share, 'rec')  141 us
    gather x1, local copies, waits for them, and re-layouts, on_device(): herd_value = jnp.take(herd_effect, local_bin)  45.5 us
    gather x1, local copies, waits for them, and re-layouts, on_device(): jnp.take(breeding, record_animal)  45.5 us
    scatter-add x1, other arithmetic, on_device(): jax.ops.segment_sum(residual, record_animal, num_segments=animals)  44 us
    unnamed x4, waiting for transfers between devices  38.5 us
    all_gather x1, waiting for transfers between devices, on_device(): breeding_block = jnp.sum(lax.all_gather(partial_value, 'rec'), axis=0)  35.8 us
    all_gather x1, blocking collectives, on_device(): breeding = lax.all_gather(breeding_block, 'ani', axis=0, tiled=True)  11.2 us
    psum x1, blocking collectives, on_device(): likelihood_grad = lax.psum(grad_part, 'ani')  9.98 us
  transfers between devices with their start and end apart: 3, of which 3 were waited for; matrix products, arithmetic and copies ran while one was open for 11% of the time, Pallas kernels for 0%

profile of v1, /device:TPU:1, one launch (start us, length us, event | category | flops | bytes accessed | tf_op | source)
XLA Modules:
  0.0 410.0 jit_solution(11379704333208392283)
XLA Ops:
  7.2 0.0 copy-start
  7.2 0.0 copy-start.2
  7.2 0.0 all-gather.3.cloned.1.call-start
  7.2 6.3 %fusion.4 = f32[1,32768]{1,0:T(1,128)} fusion(bf16[32768,128]{1,0:T(8,128)(2,1)} %param.10, f32[128]{0:T(128)} %param.11), kind=kOutput, calls=%fused_computation.13 | convolution fusion | flops 8388736 | bytes 8520192 | tf_op jit(solution)/shard_map/dot_general | solution.py:24
  13.5 0.0 all-gather.3.cloned.1.call-update
  13.6 0.0 all-reduce.6.cloned.1.call-start
  14.3 0.0 copy-done.2
  14.3 0.0 copy-done
  14.3 0.0 copy-start.3
  14.3 45.5 %gather_fusion = f32[8192]{0:T(1024)S(1)} fusion(f32[2048]{0:T(1024)S(1)} %copy-done, s32[8192]{0:T(1024)S(1)} %fusion.3), kind=kCustom, calls=%fused_computation | custom fusion | bytes 98304 | tf_op jit(solution)/shard_map/jit(_take)/gather | solution.py:30
  59.9 0.0 copy-done.3
  59.9 35.8 %all-gather.3.cloned.1.call-done = f32[1048576]{0:T(1024)} async-done(((f32[32768]{0:T(1024)}), f32[1048576]{0:T(1024)}) %all-gather.3.cloned.1.call-update) | async-done | bytes 4194320 | tf_op jit(solution)/shard_map/all_gather | solution.py:25
  95.7 5.0 %reshape.42 = f32[32,32768]{1,0:T(8,128)} reshape(f32[1048576]{0:T(1024)} %all-gather.3.cloned.1.call-done) | data formatting | bytes 8388608 | tf_op jit(solution)/shard_map/all_gather | solution.py:25
  100.7 2.6 reduce_sum.9
  103.3 11.2 %all_gather.11 = f32[131072]{0:T(1024)S(1)} all-gather(f32[32768]{0:T(1024)S(1)} %reduce_sum.9), channel_id=1, replica_groups=mesh['rec'=32,'ani'=4,'chain'=2] {'ani'}, dimensions={0}, use_global_device_ids=true | all-gather | bytes 655360 | tf_op jit(solution)/shard_map/all_gather | solution.py:26
  114.5 0.0 copy-start.4
  114.5 0.0 copy-start.8
  114.5 45.5 %gather_fusion.1 = f32[8192]{0:T(1024)S(1)} fusion(f32[131072]{0:T(1024)S(1)} %all_gather.11, s32[8192]{0:T(1024)S(1)} %fusion.2), kind=kCustom, calls=%fused_computation.1 | custom fusion | bytes 98304 | tf_op jit(solution)/shard_map/jit(_take)/gather | solution.py:32
  160.1 0.0 copy-done.4
  160.1 44.0 %scatter_custom_fusion = f32[131072]{0:T(1024)} fusion(s32[8192]{0:T(1024)S(1)} %copy-done.3, f32[8192]{0:T(1024)S(1)} %subtract_select_fusion, f32[]{:T(128)} %constant.22.clone.1), kind=kCustom, calls=%fused_computation.4 | custom fusion | flops 8192 | bytes 524292 | tf_op jit(solution)/shard_map/scatter-add | solution.py:35
  204.1 0.0 all-reduce.6.cloned.1.call-update
  204.1 0.0 all-reduce.4.cloned.1.call-start
  204.2 0.0 copy-done.8
  204.2 0.6 dynamic-slice
  205.4 38.5 %all-reduce.6.cloned.1.call-done = f32[131072]{0:T(1024)} async-done(((f32[131072]{0:T(1024)}), f32[131072]{0:T(1024)}) %all-reduce.6.cloned.1.call-update) | async-done | bytes 524304
  243.9 1.6 dynamic-slice.1
  245.4 0.0 all-reduce.4.cloned.1.call-update
  246.1 140.5 %all-reduce.4.cloned.1.call-done = f32[32768]{0:T(1024)} async-done(((f32[32768]{0:T(1024)}), f32[32768]{0:T(1024)}) %all-reduce.4.cloned.1.call-update) | async-done | bytes 131088 | tf_op jit(solution)/shard_map/psum | solution.py:37
  386.7 0.9 convert_element_type.7
  387.6 0.1 reshape.48
  387.6 0.0 copy-start.5
  387.6 0.0 copy-start.6
  387.7 0.0 copy-start.7
  387.7 0.0 copy-start.1
  387.7 4.6 %convolution_bitcast_fusion = f32[128]{0:T(128)S(1)} fusion(bf16[32768,1]{0,1:T(2,128)(2,1)S(1)} %reshape.48, bf16[32768,128]{1,0:T(8,128)(2,1)} %param.10), kind=kOutput, calls=%fused_computation.3 | convolution fusion | flops 8388608 | bytes 8454656 | tf_op jit(solution)/shard_map/dot_general | solution.py:39
  392.3 10.0 %psum.15 = f32[128]{0:T(128)S(1)} all-reduce(f32[128]{0:T(128)S(1)} %convolution_bitcast_fusion), channel_id=1, replica_groups=mesh['rec'=32,'ani'=4,'chain'=2] {'ani'}, use_global_device_ids=true, to_apply=%region_4.5 | all-reduce | flops 128 | bytes 1024 | tf_op jit(solution)/shard_map/psum | solution.py:40
  402.3 0.0 copy-done.5
  402.3 0.0 copy-done.6
  402.3 0.0 copy-done.7
  402.3 0.5 broadcast_select_fusion
  402.8 0.0 copy-done.1
  402.8 0.7 copy.16
  (3 shorter events, 0.1 us)
Async XLA Ops:
  7.2 7.1 %copy-start = (f32[2048]{0:T(1024)S(1)}, f32[2048]{0:T(1024)}, u32[]{:S(2)}) copy-start(f32[2048]{0:T(1024)} %param.15) | copy-start | bytes 24580
  7.2 7.1 %copy-start.2 = (s32[8192]{0:T(1024)S(1)}, s32[8192]{0:T(1024)}, u32[]{:S(2)}) copy-start(s32[8192]{0:T(1024)} %param.18) | copy-start | bytes 98308
  7.2 88.5 %all-gather.3.cloned.1.call-start = ((), (), s32[]{:S(2)}) async-start(), calls=%async_computation.1 | async-start | bytes 4325376 | tf_op jit(solution)/shard_map/all_gather | solution.py:25
  13.6 230.3 %all-reduce.6.cloned.1.call-start = ((), (), s32[]{:S(2)}) async-start(), calls=%async_computation.2 | async-start | bytes 1048576
  14.3 45.6 %copy-start.3 = (s32[8192]{0:T(1024)S(1)}, s32[8192]{0:T(1024)}, u32[]{:S(2)}) copy-start(s32[8192]{0:T(1024)} %param.17) | copy-start | bytes 98308
  114.5 45.5 %copy-start.4 = (f32[8192]{0:T(1024)S(1)}, f32[8192]{0:T(1024)}, u32[]{:S(2)}) copy-start(f32[8192]{0:T(1024)} %param.16) | copy-start | bytes 98308
  114.5 89.6 %copy-start.8 = (u32[256]{0:T(256)S(1)}, u32[256]{0:T(256)}, u32[]{:S(2)}) copy-start(u32[256]{0:T(256)} %constant.52) | copy-start | bytes 3076
  204.1 182.5 %all-reduce.4.cloned.1.call-start = ((), (), s32[]{:S(2)}) async-start(), calls=%async_computation | async-start | bytes 262144 | tf_op jit(solution)/shard_map/psum | solution.py:37
  387.6 14.6 %copy-start.5 = (f32[128]{0:T(128)S(1)}, f32[128]{0:T(128)}, u32[]{:S(2)}) copy-start(f32[128]{0:T(128)} %param.11) | copy-start | bytes 1540
  387.6 14.6 %copy-start.6 = (f32[128]{0:T(128)S(1)}, f32[128]{0:T(128)}, u32[]{:S(2)}) copy-start(f32[128]{0:T(128)} %param.12) | copy-start | bytes 1540
  387.7 14.6 %copy-start.7 = (f32[128]{0:T(128)S(1)}, f32[128]{0:T(128)}, u32[]{:S(2)}) copy-start(f32[128]{0:T(128)} %param.13) | copy-start | bytes 1540
  387.7 15.1 %copy-start.1 = (f32[32768]{0:T(1024)S(1)}, f32[32768]{0:T(1024)}, u32[]{:S(2)}) copy-start(f32[32768]{0:T(1024)} %all-reduce.4.cloned.1.call-done) | copy-start | bytes 393220
Sparse Core Ops, SparseCore 0:
  13.7 81.9 all-gather.2
  204.2 39.5 all-reduce.5
  247.9 138.7 all-reduce.3
